TPU v7x, 32 devices: a whole 2x2x4 slice. The times are simulated.
32 devices in a mesh: tm: 4 (over y, x), space: 8 (over z, core).
Axes of the slice: x: 2, y: 2, z: 4, core: 2. Of those that a mesh axis runs over, the one named last changes fastest.
Arguments:
- queries: bfloat16 [4, 768, 3072], P('tm', 'space'), may hold values from -8 to 8
- key_rows: bfloat16 [4, 768, 3072], P('tm', 'space'), may hold values from -8 to 8
- value_rows: bfloat16 [4, 768, 3072], P('tm', 'space'), may hold values from -6 to 6
- noise_level: int32 [4], P('tm'), may hold values from 0 to 999
- decay_power: int32 [24], replicated, may hold values from 0 to 7
- head_gain: float32 [24, 128], replicated, may hold values from 0.1 to 1.9
Outputs:
- attended: bfloat16 [4, 768, 3072], P('tm', 'space')
All inputs are finite; a program needn't handle non-finite values.
Results may differ from a plain program's by a relative error of at most 0.0049.
Values may be sent and summed in bfloat16 or wider, within the bound.
A program may use at most 64 MiB of HBM per device.

v0:
```python
import jax
import jax.numpy as jnp
from jax import lax
from jax.sharding import PartitionSpec as P

LEVELS = 1000
HGROUPS = 8
epsilon = 1e-06


def carried_in(value, axis, join, neutral):
    count, mine = (lax.axis_size(axis), lax.axis_index(axis))
    pieces = jax.tree.map(lambda part: lax.all_gather(part, axis), value)
    so_far = jax.tree.map(
        lambda part, zero: jnp.full_like(part, 0) + jnp.asarray(zero, part.dtype), value, neutral
    )

    def lap(position, so_far):
        longer = join(so_far, jax.tree.map(lambda part: part[position], pieces))
        return jax.tree.map(lambda new, old: jnp.where(position < mine, new, old), longer, so_far)

    return lax.fori_loop(0, count - 1, lap, so_far)


def spread_items(block, quarters, heads_total, depth):
    part_rows = block.shape[0] // quarters
    shaped = block.reshape(quarters, part_rows, heads_total, depth).transpose(0, 2, 1, 3)
    return shaped.reshape(quarters * heads_total, part_rows, depth)


def copied_items(block, quarters, heads_total, depth):
    every = block.reshape(block.shape[0], heads_total, depth).transpose(1, 0, 2)
    copied = jnp.broadcast_to(every[None], (quarters,) + every.shape)
    return copied.reshape(quarters * heads_total, block.shape[0], depth)


def attend_head(bundle):
    query, key_item, value_item, state, gain_row = bundle
    factor = query.shape[1] ** (-0.5)
    scores = jnp.dot(query, key_item.T, preferred_element_type=jnp.float32) * factor
    row_top = jnp.max(scores, axis=1, keepdims=True)
    weights = jnp.exp(scores - row_top)
    row_total = jnp.sum(weights, axis=1, keepdims=True)
    numerator = jnp.dot(
        weights.astype(jnp.bfloat16), value_item, preferred_element_type=jnp.float32
    )
    carried = jnp.dot(query, state, preferred_element_type=jnp.float32) * factor
    mixed = numerator / row_total + carried
    normed = mixed * lax.rsqrt(jnp.mean(mixed * mixed, axis=1, keepdims=True) + epsilon) * gain_row
    return normed.astype(jnp.bfloat16)


def compose(earlier, later):
    return (earlier[0] * later[0], later[0][:, None, None] * earlier[1] + later[1])


def body(queries, key_rows, value_rows, noise_level, decay_power, head_gain):
    heads_total = decay_power.shape[0]
    depth = head_gain.shape[1]
    local_rows = queries.shape[1]
    quarters = lax.axis_size("space") // HGROUPS
    grouped = heads_total // HGROUPS
    query_items = spread_items(queries[0], quarters, heads_total, depth)
    keys_sent = copied_items(key_rows[0], quarters, heads_total, depth)
    values_sent = copied_items(value_rows[0], quarters, heads_total, depth)
    query_got, keys_got, values_got = (
        lax.all_to_all(query_items, "space", split_axis=0, concat_axis=1, tiled=True),
        lax.all_to_all(keys_sent, "space", split_axis=0, concat_axis=1, tiled=True),
        lax.all_to_all(values_sent, "space", split_axis=0, concat_axis=1, tiled=True),
    )
    key_count = keys_got.shape[1]
    fresh = (
        jnp.einsum("inh,ine->ihe", keys_got, values_got, preferred_element_type=jnp.float32)
        / key_count
    )
    group_index = lax.axis_index("space") % HGROUPS
    powers = lax.dynamic_slice_in_dim(decay_power, group_index * grouped, grouped).astype(
        jnp.float32
    )
    level_now = noise_level[0].astype(jnp.float32)
    block_count = lax.axis_size("tm")
    rate = jnp.exp2(-(powers * (0.25 + 1.75 * level_now / LEVELS)) / block_count)
    zeros_state = jnp.zeros_like(fresh)
    unused_rate, before = carried_in(
        (rate, fresh), "tm", compose, (jnp.ones_like(rate), zeros_state)
    )
    state = (rate[:, None, None] * before).astype(jnp.bfloat16)
    gain_rows = lax.dynamic_slice_in_dim(head_gain, group_index * grouped, grouped)
    outcome = lax.map(attend_head, (query_got, keys_got, values_got, state, gain_rows))
    returned = lax.all_to_all(outcome, "space", split_axis=1, concat_axis=0, tiled=True)
    part_rows = local_rows // quarters
    restored = returned.reshape(quarters, heads_total, part_rows, depth).transpose(0, 2, 1, 3)
    return restored.reshape(1, local_rows, heads_total * depth)


def solution(mesh):
    in_specs = (
        P("tm", "space", None),
        P("tm", "space", None),
        P("tm", "space", None),
        P("tm"),
        P(),
        P(),
    )
    out_specs = P("tm", "space", None)
    return jax.shard_map(body, mesh=mesh, in_specs=in_specs, out_specs=out_specs, check_vma=False)
```

profile of v0, /device:TPU:0, one launch (start us, length us, event | category | flops | bytes accessed | tf_op | source)
XLA Modules:
  0.0 99.5 jit_solution(8693053812802755996)
XLA Ops:
  0.0 0.0 copy-start
  0.0 0.0 copy-start.1
  0.0 1.2 %copy.38 = bf16[12,8,24,128]{3,2,1,0:T(8,128)(2,1)S(1)} copy(bf16[12,8,24,128]{3,1,2,0:T(8,128)(2,1)} %bitcast.111) | data formatting | bytes 1179648
  1.2 0.9 copy.26
  2.1 0.0 copy-start.4
  2.1 0.0 copy-start.3
  2.2 0.0 copy-start.2
  2.2 6.5 %all-to-all-start.1 = ((bf16[24,96,128]{2,1,0:T(8,128)(2,1)}), bf16[24,96,128]{2,1,0:T(8,128)(2,1)S(1)}, u32[]{:S(2)}, u32[]{:S(2)}) async-start(bf16[24,96,128]{2,1,0:T(8,128)(2,1)} %copy.26), calls=%async_computation.1 | async-start | bytes 1179648 | tf_op jit(solution)/shard_map/all_to_all | solution.py:68
  8.6 0.0 copy-done.1
  8.6 0.1 copy.39
  8.8 0.9 copy.28
  9.7 15.7 %all-to-all-done.1 = bf16[24,96,128]{2,1,0:T(8,128)(2,1)S(1)} async-done(((bf16[24,96,128]{2,1,0:T(8,128)(2,1)}), bf16[24,96,128]{2,1,0:T(8,128)(2,1)S(1)}, u32[]{:S(2)}, u32[]{:S(2)}) %all-to-all-start.1) | async-done | bytes 589856 | tf_op jit(solution)/shard_map/all_to_all | solution.py:68
  25.4 3.5 %all-to-all-start.2 = ((bf16[24,96,128]{2,1,0:T(8,128)(2,1)}), bf16[24,96,128]{2,1,0:T(8,128)(2,1)S(1)}, u32[]{:S(2)}, u32[]{:S(2)}) async-start(bf16[24,96,128]{2,1,0:T(8,128)(2,1)} %copy.28), calls=%async_computation.2 | async-start | bytes 1179648 | tf_op jit(solution)/shard_map/all_to_all | solution.py:69
  29.6 0.0 copy-done.4
  29.6 0.6 dynamic-slice
  30.9 0.0 copy-done.3
  30.9 0.2 fusion.25
  31.0 9.9 %all-reduce = f32[12]{0:T(128)S(1)} all-reduce(f32[12]{0:T(128)S(1)} %get-tuple-element.187), channel_id=2, replica_groups=mesh['tm'=4,'space'=8] {'tm'}, use_global_device_ids=true, to_apply=%add | all-reduce | flops 12 | bytes 96
  40.9 0.1 reshape.30
  41.0 0.0 copy-done.2
  41.0 0.1 copy.37
  41.1 0.1 bitcast_bitcast_fusion
  41.2 0.9 copy.24
  42.1 0.0 copy-done
  42.2 3.4 %all-to-all-done.2 = bf16[24,96,128]{2,1,0:T(8,128)(2,1)S(1)} async-done(((bf16[24,96,128]{2,1,0:T(8,128)(2,1)}), bf16[24,96,128]{2,1,0:T(8,128)(2,1)S(1)}, u32[]{:S(2)}, u32[]{:S(2)}) %all-to-all-start.2) | async-done | bytes 589856 | tf_op jit(solution)/shard_map/all_to_all | solution.py:69
  45.6 3.5 %all-to-all-start = ((bf16[24,96,128]{2,1,0:T(8,128)(2,1)}), bf16[24,96,128]{2,1,0:T(8,128)(2,1)S(1)}, u32[]{:S(2)}, u32[]{:S(2)}) async-start(bf16[24,96,128]{2,1,0:T(8,128)(2,1)} %copy.24), calls=%async_computation | async-start | bytes 1179648 | tf_op jit(solution)/shard_map/all_to_all | solution.py:67
  49.2 0.4 convolution_multiply_fusion.1
  49.5 12.5 %all-gather.1 = f32[12,128,128]{2,1,0:T(8,128)S(1)} all-gather(f32[3,128,128]{2,1,0:T(8,128)S(1)} %convolution_multiply_fusion.1), channel_id=3, replica_groups=mesh['tm'=4,'space'=8] {'tm'}, dimensions={0}, use_global_device_ids=true | all-gather | bytes 983040 | tf_op jit(solution)/shard_map/all_gather | solution.py:13
  62.1 0.4 while.25
  62.1 0.1 fusion.39
  62.2 0.1 fusion.39
  62.4 0.1 fusion.39
  62.5 3.3 %all-to-all-done = bf16[24,96,128]{2,1,0:T(8,128)(2,1)S(1)} async-done(((bf16[24,96,128]{2,1,0:T(8,128)(2,1)}), bf16[24,96,128]{2,1,0:T(8,128)(2,1)S(1)}, u32[]{:S(2)}, u32[]{:S(2)}) %all-to-all-start) | async-done | bytes 589856 | tf_op jit(solution)/shard_map/all_to_all | solution.py:67
  65.8 0.1 multiply_convert_fusion.1
  65.9 7.7 %while.24 = (s32[]{:T(128)}, bf16[3,768,128]{1,2,0:T(8,128)(2,1)}, bf16[3,768,128]{2,1,0:T(8,128)(2,1)S(1)}, bf16[3,768,128]{2,1,0:T(8,128)(2,1)S(1)}, bf16[3,76...) while((s32[]{:T(128)}, bf16[3,768,128]{1,2,0:T(8,128)(2,1)}, ...), condition=%wide.region_6.7_spmd, body=%wide.region_2.6_spmd.sunk | while | flops 332659968 | bytes 9700445 | solution.py:89
  65.9 0.5 multiply_reduce_fusion.4
  66.4 0.4 fusion.36
  66.8 0.2 convolution_multiply_fusion.3
  67.1 0.6 multiply_reduce_fusion.5
  67.7 0.8 fusion.38
  68.5 0.5 multiply_reduce_fusion.4
  69.0 0.4 fusion.36
  69.4 0.3 convolution_multiply_fusion.3
  69.7 0.6 multiply_reduce_fusion.5
  70.3 0.8 fusion.38
  71.0 0.5 multiply_reduce_fusion.4
  71.5 0.4 fusion.36
  71.9 0.3 convolution_multiply_fusion.3
  72.2 0.6 multiply_reduce_fusion.5
  72.8 0.8 fusion.38
  73.6 1.5 %copy.31 = bf16[3,768,128]{2,0,1:T(4,128)(2,1)S(1)} copy(bf16[3,768,128]{1,2,0:T(8,128)(2,1)} %get-tuple-element.137) | data formatting | bytes 1179648 | tf_op jit(solution)/shard_map/while | solution.py:89
  75.1 23.4 %all_to_all.69 = bf16[3,768,128]{2,0,1:T(4,128)(2,1)S(1)} all-to-all(bf16[3,768,128]{2,0,1:T(4,128)(2,1)S(1)} %copy.31), channel_id=1, replica_groups=mesh['tm'=4,'space'=8] {'space'}, dimensions={1} | all-to-all | bytes 1179648 | tf_op jit(solution)/shard_map/all_to_all | solution.py:90
  98.4 0.1 copy.32
  98.6 1.0 copy.41
  (17 shorter events, 0.3 us)
Async XLA Ops:
  0.0 42.1 %copy-start = (f32[24,128]{1,0:T(8,128)S(1)}, f32[24,128]{1,0:T(8,128)}, u32[]{:S(2)}) copy-start(f32[24,128]{1,0:T(8,128)} %param.15) | copy-start | bytes 36868
  0.0 8.6 %copy-start.1 = (bf16[1,96,3072]{2,1,0:T(8,128)(2,1)S(1)}, bf16[1,96,3072]{2,1,0:T(8,128)(2,1)}, u32[]{:S(2)}) copy-start(bf16[1,96,3072]{2,1,0:T(8,128)(2,1)} %param.12) | copy-start | bytes 1769476
  2.1 27.4 %copy-start.4 = (u32[32]{0:T(128)S(1)}, u32[32]{0:T(128)}, u32[]{:S(2)}) copy-start(u32[32]{0:T(128)} %constant.102) | copy-start | bytes 388
  2.1 28.7 %copy-start.3 = (s32[24]{0:T(128)S(1)}, s32[24]{0:T(128)}, u32[]{:S(2)}) copy-start(s32[24]{0:T(128)} %param.14) | copy-start | bytes 292
  2.2 38.9 %copy-start.2 = (bf16[1,96,3072]{2,1,0:T(8,128)(2,1)S(1)}, bf16[1,96,3072]{2,1,0:T(8,128)(2,1)}, u32[]{:S(2)}) copy-start(bf16[1,96,3072]{2,1,0:T(8,128)(2,1)} %param.10) | copy-start | bytes 1769476
  2.2 23.2 %all-to-all-start.1 = ((bf16[24,96,128]{2,1,0:T(8,128)(2,1)}), bf16[24,96,128]{2,1,0:T(8,128)(2,1)S(1)}, u32[]{:S(2)}, u32[]{:S(2)}) async-start(bf16[24,96,128]{2,1,0:T(8,128)(2,1)} %copy.26), calls=%async_computation.1 | async-start | bytes 1179648 | tf_op jit(solution)/shard_map/all_to_all | solution.py:68
  25.4 20.2 %all-to-all-start.2 = ((bf16[24,96,128]{2,1,0:T(8,128)(2,1)}), bf16[24,96,128]{2,1,0:T(8,128)(2,1)S(1)}, u32[]{:S(2)}, u32[]{:S(2)}) async-start(bf16[24,96,128]{2,1,0:T(8,128)(2,1)} %copy.28), calls=%async_computation.2 | async-start | bytes 1179648 | tf_op jit(solution)/shard_map/all_to_all | solution.py:69
  45.6 20.2 %all-to-all-start = ((bf16[24,96,128]{2,1,0:T(8,128)(2,1)}), bf16[24,96,128]{2,1,0:T(8,128)(2,1)S(1)}, u32[]{:S(2)}, u32[]{:S(2)}) async-start(bf16[24,96,128]{2,1,0:T(8,128)(2,1)} %copy.24), calls=%async_computation | async-start | bytes 1179648 | tf_op jit(solution)/shard_map/all_to_all | solution.py:67
where the time goes:
time: 100 us; the launch traced here: 99.5 us
  blocking collectives  45.8 us (46%)
  waiting for transfers between devices  22.4 us (22%)
  starting transfers between devices  13.6 us (14%)
  local copies, waits for them, and re-layouts  7.68 us (8%)
  matrix products  4.3 us (4%)
  other arithmetic  4.18 us (4%)
  between operations  1.48 us (1%)
    all_to_all x1, blocking collectives, body(): lax.all_to_all(outcome, 'space', split_axis=1, concat_axis=0, tiled=True)  23.4 us
    all_to_all x1, waiting for transfers between devices, body(): lax.all_to_all(keys_sent, 'space', split_axis=0, concat_axis=1, tiled=True)  15.7 us
    all_gather x1, blocking collectives, carried_in(): pieces = jax.tree.map(lambda part: lax.all_gather(part, axis), value)  12.5 us
    unnamed x1, blocking collectives  9.88 us
    all_to_all x1, starting transfers between devices, body(): lax.all_to_all(keys_sent, 'space', split_axis=0, concat_axis=1, tiled=True)  6.49 us
    all_to_all x1, starting transfers between devices, body(): lax.all_to_all(values_sent, 'space', split_axis=0, concat_axis=1, tiled=T...  3.54 us
    all_to_all x1, starting transfers between devices, body(): lax.all_to_all(query_items, 'space', split_axis=0, concat_axis=1, tiled=T...  3.54 us
    all_to_all x1, waiting for transfers between devices, body(): lax.all_to_all(values_sent, 'space', split_axis=0, concat_axis=1, tiled=T...  3.4 us
  transfers between devices with their start and end apart: 3, of which 3 were waited for; matrix products, arithmetic and copies ran while one was open for 4% of the time, Pallas kernels for 0%

commit v1 on v0

--- a/solution.py
+++ b/solution.py
@@ -6,6 +6,18 @@
 LEVELS = 1000
 HGROUPS = 8
 epsilon = 1e-06
+
+
+def cut_along(value, dim, size):
+    shape = value.shape
+    blocks = value.reshape(*shape[:dim], size, shape[dim] // size, *shape[dim + 1 :])
+    return jnp.moveaxis(blocks, dim, 0)
+
+
+def joined_along(blocks, dim):
+    dims = list(blocks.shape[1:])
+    dims[dim] *= blocks.shape[0]
+    return jnp.moveaxis(blocks, 0, dim).reshape(dims)
 
 
 def carried_in(value, axis, join, neutral):
@@ -87,7 +99,14 @@
     state = (rate[:, None, None] * before).astype(jnp.bfloat16)
     gain_rows = lax.dynamic_slice_in_dim(head_gain, group_index * grouped, grouped)
     outcome = lax.map(attend_head, (query_got, keys_got, values_got, state, gain_rows))
-    returned = lax.all_to_all(outcome, "space", split_axis=1, concat_axis=0, tiled=True)
+    peers, index = (lax.axis_size("space"), lax.axis_index("space"))
+    parts = cut_along(outcome, 1, peers)
+    outs = [parts[index]]
+    for hop in range(1, peers):
+        sent = parts[(index + hop) % peers]
+        outs.append(lax.ppermute(sent, "space", [(i, (i + hop) % peers) for i in range(peers)]))
+    parts = jnp.stack(outs)[(index - jnp.arange(peers)) % peers]
+    returned = joined_along(parts, 0)
     part_rows = local_rows // quarters
     restored = returned.reshape(quarters, heads_total, part_rows, depth).transpose(0, 2, 1, 3)
     return restored.reshape(1, local_rows, heads_total * depth)

time: 100 us -> 92.5 us (0.925)
  the two profiles are of different devices: /device:TPU:0 before, /device:TPU:13 now
where the time goes in v1:
time: 92.5 us; the launch traced here: 91.9 us
  starting transfers between devices  29.8 us (32%)
  waiting for transfers between devices  24.8 us (27%)
  blocking collectives  17.7 us (19%)
  local copies, waits for them, and re-layouts  11.4 us (12%)
  matrix products  4.29 us (5%)
  other arithmetic  2.15 us (2%)
  between operations  1.6 us (2%)
    all_to_all x1, waiting for transfers between devices, body(): lax.all_to_all(keys_sent, 'space', split_axis=0, concat_axis=1, tiled=True)  12.2 us
    all_gather x1, blocking collectives, carried_in(): pieces = jax.tree.map(lambda part: lax.all_gather(part, axis), value)  10.5 us
    ppermute x7, starting transfers between devices, body(): lax.ppermute(sent, 'space', [(i, (i + hop) % peers) for i in range(peers)])  10.2 us
    ppermute x7, waiting for transfers between devices, body(): lax.ppermute(sent, 'space', [(i, (i + hop) % peers) for i in range(peers)])  8.11 us
    unnamed x1, blocking collectives  7.16 us
    all_to_all x1, starting transfers between devices, body(): lax.all_to_all(query_items, 'space', split_axis=0, concat_axis=1, tiled=T...  6.98 us
    all_to_all x1, starting transfers between devices, body(): lax.all_to_all(values_sent, 'space', split_axis=0, concat_axis=1, tiled=T...  6.95 us
    all_to_all x1, starting transfers between devices, body(): lax.all_to_all(keys_sent, 'space', split_axis=0, concat_axis=1, tiled=True)  5.74 us
  transfers between devices with their start and end apart: 10, of which 6 were waited for; matrix products, arithmetic and copies ran while one was open for 5% of the time, Pallas kernels for 0%

profile of v1, /device:TPU:13, one launch (start us, length us, event | category | flops | bytes accessed | tf_op | source)
XLA Modules:
  0.0 91.9 jit_solution(4627879809685101602)
XLA Ops:
  0.0 1.2 %copy.35 = bf16[12,8,24,128]{3,2,1,0:T(8,128)(2,1)S(1)} copy(bf16[12,8,24,128]{3,1,2,0:T(8,128)(2,1)} %bitcast.138) | data formatting | bytes 1179648
  1.2 0.9 copy.23
  2.2 5.7 %all-to-all-start.1 = ((bf16[24,96,128]{2,1,0:T(8,128)(2,1)}), bf16[24,96,128]{2,1,0:T(8,128)(2,1)S(1)}, u32[]{:S(2)}, u32[]{:S(2)}) async-start(bf16[24,96,128]{2,1,0:T(8,128)(2,1)} %copy.23), calls=%async_computation.1 | async-start | bytes 1179648 | tf_op jit(solution)/shard_map/all_to_all | solution.py:80
  7.9 0.1 copy.36
  8.0 0.9 copy.25
  8.9 12.2 %all-to-all-done.1 = bf16[24,96,128]{2,1,0:T(8,128)(2,1)S(1)} async-done(((bf16[24,96,128]{2,1,0:T(8,128)(2,1)}), bf16[24,96,128]{2,1,0:T(8,128)(2,1)S(1)}, u32[]{:S(2)}, u32[]{:S(2)}) %all-to-all-start.1) | async-done | bytes 589856 | tf_op jit(solution)/shard_map/all_to_all | solution.py:80
  21.1 7.0 %all-to-all-start.2 = ((bf16[24,96,128]{2,1,0:T(8,128)(2,1)}), bf16[24,96,128]{2,1,0:T(8,128)(2,1)S(1)}, u32[]{:S(2)}, u32[]{:S(2)}) async-start(bf16[24,96,128]{2,1,0:T(8,128)(2,1)} %copy.25), calls=%async_computation.2 | async-start | bytes 1179648 | tf_op jit(solution)/shard_map/all_to_all | solution.py:81
  28.7 0.6 dynamic-slice.32
  30.0 0.2 fusion.26
  30.2 7.2 %all-reduce = f32[12]{0:T(128)S(1)} all-reduce(f32[12]{0:T(128)S(1)} %get-tuple-element.187), channel_id=2, replica_groups=mesh['tm'=4,'space'=8] {'tm'}, use_global_device_ids=true, to_apply=%add | all-reduce | flops 12 | bytes 96
  37.4 0.1 reshape.101
  37.5 0.1 copy.34
  37.6 0.1 bitcast_bitcast_fusion
  37.7 0.9 copy.21
  38.7 2.6 %all-to-all-done.2 = bf16[24,96,128]{2,1,0:T(8,128)(2,1)S(1)} async-done(((bf16[24,96,128]{2,1,0:T(8,128)(2,1)}), bf16[24,96,128]{2,1,0:T(8,128)(2,1)S(1)}, u32[]{:S(2)}, u32[]{:S(2)}) %all-to-all-start.2) | async-done | bytes 589856 | tf_op jit(solution)/shard_map/all_to_all | solution.py:81
  41.3 7.0 %all-to-all-start = ((bf16[24,96,128]{2,1,0:T(8,128)(2,1)}), bf16[24,96,128]{2,1,0:T(8,128)(2,1)S(1)}, u32[]{:S(2)}, u32[]{:S(2)}) async-start(bf16[24,96,128]{2,1,0:T(8,128)(2,1)} %copy.21), calls=%async_computation | async-start | bytes 1179648 | tf_op jit(solution)/shard_map/all_to_all | solution.py:79
  48.3 0.4 convolution_multiply_fusion.1
  48.7 10.5 %all-gather.1 = f32[12,128,128]{2,1,0:T(8,128)S(1)} all-gather(f32[3,128,128]{2,1,0:T(8,128)S(1)} %convolution_multiply_fusion.1), channel_id=3, replica_groups=mesh['tm'=4,'space'=8] {'tm'}, dimensions={0}, use_global_device_ids=true | all-gather | bytes 983040 | tf_op jit(solution)/shard_map/all_gather | solution.py:25
  59.2 0.4 while.25
  59.2 0.1 fusion.40
  59.4 0.1 fusion.40
  59.5 0.1 fusion.40
  59.6 1.9 %all-to-all-done = bf16[24,96,128]{2,1,0:T(8,128)(2,1)S(1)} async-done(((bf16[24,96,128]{2,1,0:T(8,128)(2,1)}), bf16[24,96,128]{2,1,0:T(8,128)(2,1)S(1)}, u32[]{:S(2)}, u32[]{:S(2)}) %all-to-all-start) | async-done | bytes 589856 | tf_op jit(solution)/shard_map/all_to_all | solution.py:79
  61.6 0.1 multiply_convert_fusion.1
  61.6 8.2 %while.24 = (s32[]{:T(128)}, bf16[3,768,128]{2,1,0:T(8,128)(2,1)}, bf16[3,768,128]{2,1,0:T(8,128)(2,1)S(1)}, bf16[3,768,128]{2,1,0:T(8,128)(2,1)S(1)}, bf16[3,76...) while((s32[]{:T(128)}, bf16[3,768,128]{2,1,0:T(8,128)(2,1)}, ...), condition=%wide.region_6.7_spmd, body=%wide.region_2.6_spmd.sunk | while | flops 332659968 | bytes 10486877 | solution.py:101
  61.7 0.5 multiply_reduce_fusion.4
  62.1 0.4 fusion.37
  62.6 0.3 convolution_multiply_fusion.3
  62.8 0.6 multiply_reduce_fusion.5
  63.4 0.1 fusion.39
  63.5 0.2 copy.40
  63.7 0.7 constant_dynamic-update-slice_fusion.2
  64.4 0.5 multiply_reduce_fusion.4
  64.9 0.4 fusion.37
  65.3 0.2 convolution_multiply_fusion.3
  65.6 0.6 multiply_reduce_fusion.5
  66.2 0.1 fusion.39
  66.3 0.2 copy.40
  66.4 0.7 constant_dynamic-update-slice_fusion.2
  67.1 0.5 multiply_reduce_fusion.4
  67.6 0.4 fusion.37
  68.0 0.3 convolution_multiply_fusion.3
  68.3 0.6 multiply_reduce_fusion.5
  68.9 0.1 fusion.39
  69.0 0.2 copy.40
  69.2 0.7 constant_dynamic-update-slice_fusion.2
  69.9 1.1 %dynamic-slice_bitcast_fusion.1 = (bf16[3,96,128]{2,1,0:T(8,128)(2,1)S(1)}, bf16[3,96,128]{2,1,0:T(8,128)(2,1)S(1)}, bf16[3,96,128]{2,1,0:T(8,128)(2,1)S(1)}, bf...) fusion(bf16[3,8,96,128]{3,2,1,0:T(8,128)(2,1)} %bitcast.141, ...), kind=kLoop, calls=%fused_computation.47 | loop fusion | bytes 1032220 | tf_op jit(solution)/shard_map/squeeze | solution.py:106
  71.0 1.8 %collective-permute-start = (bf16[3,96,128]{2,1,0:T(8,128)(2,1)S(1)}, bf16[3,96,128]{2,1,0:T(8,128)(2,1)S(1)}, u32[]{:S(2)}, u32[]{:S(2)}) collective-permute-start(bf16[3,96,128]{2,1,0:T(8,128)(2,1)S(1)} %get-tuple-element.199), channel_id=1, source_target_pairs={{0,1},{1,2},{2,3},{3,4},{4,5},{5,6},{6,7},{7,0},{8,9},{9,10},{10,1... | collective-permute-start | bytes 221192 | tf_op jit(solution)/shard_map/ppermute | solution.py:107
  72.8 1.9 %collective-permute-start.1 = (bf16[3,96,128]{2,1,0:T(8,128)(2,1)S(1)}, bf16[3,96,128]{2,1,0:T(8,128)(2,1)S(1)}, u32[]{:S(2)}, u32[]{:S(2)}) collective-permute-start(bf16[3,96,128]{2,1,0:T(8,128)(2,1)S(1)} %get-tuple-element.198), channel_id=1, source_target_pairs={{0,2},{1,3},{2,4},{3,5},{4,6},{5,7},{6,0},{7,1},{8,10},{9,11},{10,... | collective-permute-start | bytes 221192 | tf_op jit(solution)/shard_map/ppermute | solution.py:107
  74.7 2.4 %collective-permute-start.2 = (bf16[3,96,128]{2,1,0:T(8,128)(2,1)S(1)}, bf16[3,96,128]{2,1,0:T(8,128)(2,1)S(1)}, u32[]{:S(2)}, u32[]{:S(2)}) collective-permute-start(bf16[3,96,128]{2,1,0:T(8,128)(2,1)S(1)} %get-tuple-element.197), channel_id=1, source_target_pairs={{0,3},{1,4},{2,5},{3,6},{4,7},{5,0},{6,1},{7,2},{8,11},{9,12},{10,... | collective-permute-start | bytes 221192 | tf_op jit(solution)/shard_map/ppermute | solution.py:107
  77.0 0.0 collective-permute-start.3
  77.0 1.7 %collective-permute-start.4 = (bf16[3,96,128]{2,1,0:T(8,128)(2,1)S(1)}, bf16[3,96,128]{2,1,0:T(8,128)(2,1)S(1)}, u32[]{:S(2)}, u32[]{:S(2)}) collective-permute-start(bf16[3,96,128]{2,1,0:T(8,128)(2,1)S(1)} %get-tuple-element.195), channel_id=1, source_target_pairs={{0,5},{1,6},{2,7},{3,0},{4,1},{5,2},{6,3},{7,4},{8,13},{9,14},{10,... | collective-permute-start | bytes 221192 | tf_op jit(solution)/shard_map/ppermute | solution.py:107
  78.7 0.9 bitcast_dynamic-update-slice_fusion.7
  79.6 0.0 collective-permute-done
  79.6 2.4 %collective-permute-start.5 = (bf16[3,96,128]{2,1,0:T(8,128)(2,1)S(1)}, bf16[3,96,128]{2,1,0:T(8,128)(2,1)S(1)}, u32[]{:S(2)}, u32[]{:S(2)}) collective-permute-start(bf16[3,96,128]{2,1,0:T(8,128)(2,1)S(1)} %get-tuple-element.194), channel_id=1, source_target_pairs={{0,6},{1,7},{2,0},{3,1},{4,2},{5,3},{6,4},{7,5},{8,14},{9,15},{10,... | collective-permute-start | bytes 221192 | tf_op jit(solution)/shard_map/ppermute | solution.py:107
  82.0 0.0 collective-permute-done.1
  82.0 0.1 collective-permute-start.6
  82.1 0.0 collective-permute-done.2
  82.1 3.6 %collective-permute-done.3 = bf16[3,96,128]{2,1,0:T(8,128)(2,1)S(1)} collective-permute-done((bf16[3,96,128]{2,1,0:T(8,128)(2,1)S(1)}, bf16[3,96,128]{2,1,0:T(8,128)(2,1)S(1)}, u32[]{:S(2)}, u32[]{:S(2)}) %collective-permute-start.3) | collective-permute-done | bytes 73760 | tf_op jit(solution)/shard_map/ppermute | solution.py:107
  85.7 0.0 collective-permute-done.4
  85.7 4.5 %collective-permute-done.5 = bf16[3,96,128]{2,1,0:T(8,128)(2,1)S(1)} collective-permute-done((bf16[3,96,128]{2,1,0:T(8,128)(2,1)S(1)}, bf16[3,96,128]{2,1,0:T(8,128)(2,1)S(1)}, u32[]{:S(2)}, u32[]{:S(2)}) %collective-permute-start.5) | collective-permute-done | bytes 73760 | tf_op jit(solution)/shard_map/ppermute | solution.py:107
  90.2 0.1 collective-permute-done.6
  90.3 0.7 gather_fusion
  91.0 1.0 %copy.38 = bf16[1,24,12,8,128]{4,3,1,2,0:T(8,128)(2,1)} copy(bf16[1,24,12,8,128]{4,3,2,1,0:T(8,128)(2,1)S(1)} %bitcast.132) | data formatting | bytes 1179648 | tf_op jit(solution)/shard_map/reshape | solution.py:112
  (35 shorter events, 0.4 us)
Async XLA Ops:
  0.0 38.6 %copy-start = (f32[24,128]{1,0:T(8,128)S(1)}, f32[24,128]{1,0:T(8,128)}, u32[]{:S(2)}) copy-start(f32[24,128]{1,0:T(8,128)} %param.15) | copy-start | bytes 36868
  0.0 7.9 %copy-start.1 = (bf16[1,96,3072]{2,1,0:T(8,128)(2,1)S(1)}, bf16[1,96,3072]{2,1,0:T(8,128)(2,1)}, u32[]{:S(2)}) copy-start(bf16[1,96,3072]{2,1,0:T(8,128)(2,1)} %param.12) | copy-start | bytes 1769476
  2.1 26.6 %copy-start.4 = (u32[32]{0:T(128)S(1)}, u32[32]{0:T(128)}, u32[]{:S(2)}) copy-start(u32[32]{0:T(128)} %constant.151) | copy-start | bytes 388
  2.1 27.9 %copy-start.3 = (s32[24]{0:T(128)S(1)}, s32[24]{0:T(128)}, u32[]{:S(2)}) copy-start(s32[24]{0:T(128)} %param.14) | copy-start | bytes 292
  2.2 35.4 %copy-start.2 = (bf16[1,96,3072]{2,1,0:T(8,128)(2,1)S(1)}, bf16[1,96,3072]{2,1,0:T(8,128)(2,1)}, u32[]{:S(2)}) copy-start(bf16[1,96,3072]{2,1,0:T(8,128)(2,1)} %param.10) | copy-start | bytes 1769476
  2.2 19.0 %all-to-all-start.1 = ((bf16[24,96,128]{2,1,0:T(8,128)(2,1)}), bf16[24,96,128]{2,1,0:T(8,128)(2,1)S(1)}, u32[]{:S(2)}, u32[]{:S(2)}) async-start(bf16[24,96,128]{2,1,0:T(8,128)(2,1)} %copy.23), calls=%async_computation.1 | async-start | bytes 1179648 | tf_op jit(solution)/shard_map/all_to_all | solution.py:80
  21.1 20.2 %all-to-all-start.2 = ((bf16[24,96,128]{2,1,0:T(8,128)(2,1)}), bf16[24,96,128]{2,1,0:T(8,128)(2,1)S(1)}, u32[]{:S(2)}, u32[]{:S(2)}) async-start(bf16[24,96,128]{2,1,0:T(8,128)(2,1)} %copy.25), calls=%async_computation.2 | async-start | bytes 1179648 | tf_op jit(solution)/shard_map/all_to_all | solution.py:81
  41.3 20.2 %all-to-all-start = ((bf16[24,96,128]{2,1,0:T(8,128)(2,1)}), bf16[24,96,128]{2,1,0:T(8,128)(2,1)S(1)}, u32[]{:S(2)}, u32[]{:S(2)}) async-start(bf16[24,96,128]{2,1,0:T(8,128)(2,1)} %copy.21), calls=%async_computation | async-start | bytes 1179648 | tf_op jit(solution)/shard_map/all_to_all | solution.py:79
  71.0 8.6 %collective-permute-start = (bf16[3,96,128]{2,1,0:T(8,128)(2,1)S(1)}, bf16[3,96,128]{2,1,0:T(8,128)(2,1)S(1)}, u32[]{:S(2)}, u32[]{:S(2)}) collective-permute-start(bf16[3,96,128]{2,1,0:T(8,128)(2,1)S(1)} %get-tuple-element.199), channel_id=1, source_target_pairs={{0,1},{1,2},{2,3},{3,4},{4,5},{5,6},{6,7},{7,0},{8,9},{9,10},{10,1... | collective-permute-start | bytes 221192 | tf_op jit(solution)/shard_map/ppermute | solution.py:107
  72.8 9.3 %collective-permute-start.1 = (bf16[3,96,128]{2,1,0:T(8,128)(2,1)S(1)}, bf16[3,96,128]{2,1,0:T(8,128)(2,1)S(1)}, u32[]{:S(2)}, u32[]{:S(2)}) collective-permute-start(bf16[3,96,128]{2,1,0:T(8,128)(2,1)S(1)} %get-tuple-element.198), channel_id=1, source_target_pairs={{0,2},{1,3},{2,4},{3,5},{4,6},{5,7},{6,0},{7,1},{8,10},{9,11},{10,... | collective-permute-start | bytes 221192 | tf_op jit(solution)/shard_map/ppermute | solution.py:107
  74.7 7.5 %collective-permute-start.2 = (bf16[3,96,128]{2,1,0:T(8,128)(2,1)S(1)}, bf16[3,96,128]{2,1,0:T(8,128)(2,1)S(1)}, u32[]{:S(2)}, u32[]{:S(2)}) collective-permute-start(bf16[3,96,128]{2,1,0:T(8,128)(2,1)S(1)} %get-tuple-element.197), channel_id=1, source_target_pairs={{0,3},{1,4},{2,5},{3,6},{4,7},{5,0},{6,1},{7,2},{8,11},{9,12},{10,... | collective-permute-start | bytes 221192 | tf_op jit(solution)/shard_map/ppermute | solution.py:107
  77.0 8.7 %collective-permute-start.3 = (bf16[3,96,128]{2,1,0:T(8,128)(2,1)S(1)}, bf16[3,96,128]{2,1,0:T(8,128)(2,1)S(1)}, u32[]{:S(2)}, u32[]{:S(2)}) collective-permute-start(bf16[3,96,128]{2,1,0:T(8,128)(2,1)S(1)} %get-tuple-element.196), channel_id=1, source_target_pairs={{0,4},{1,5},{2,6},{3,7},{4,0},{5,1},{6,2},{7,3},{8,12},{9,13},{10,... | collective-permute-start | bytes 221192 | tf_op jit(solution)/shard_map/ppermute | solution.py:107
  77.0 8.7 %collective-permute-start.4 = (bf16[3,96,128]{2,1,0:T(8,128)(2,1)S(1)}, bf16[3,96,128]{2,1,0:T(8,128)(2,1)S(1)}, u32[]{:S(2)}, u32[]{:S(2)}) collective-permute-start(bf16[3,96,128]{2,1,0:T(8,128)(2,1)S(1)} %get-tuple-element.195), channel_id=1, source_target_pairs={{0,5},{1,6},{2,7},{3,0},{4,1},{5,2},{6,3},{7,4},{8,13},{9,14},{10,... | collective-permute-start | bytes 221192 | tf_op jit(solution)/shard_map/ppermute | solution.py:107
  79.6 10.6 %collective-permute-start.5 = (bf16[3,96,128]{2,1,0:T(8,128)(2,1)S(1)}, bf16[3,96,128]{2,1,0:T(8,128)(2,1)S(1)}, u32[]{:S(2)}, u32[]{:S(2)}) collective-permute-start(bf16[3,96,128]{2,1,0:T(8,128)(2,1)S(1)} %get-tuple-element.194), channel_id=1, source_target_pairs={{0,6},{1,7},{2,0},{3,1},{4,2},{5,3},{6,4},{7,5},{8,14},{9,15},{10,... | collective-permute-start | bytes 221192 | tf_op jit(solution)/shard_map/ppermute | solution.py:107
  82.0 8.3 %collective-permute-start.6 = (bf16[3,96,128]{2,1,0:T(8,128)(2,1)S(1)}, bf16[3,96,128]{2,1,0:T(8,128)(2,1)S(1)}, u32[]{:S(2)}, u32[]{:S(2)}) collective-permute-start(bf16[3,96,128]{2,1,0:T(8,128)(2,1)S(1)} %get-tuple-element.193), channel_id=1, source_target_pairs={{0,7},{1,0},{2,1},{3,2},{4,3},{5,4},{6,5},{7,6},{8,15},{9,8},{10,9... | collective-permute-start | bytes 221192 | tf_op jit(solution)/shard_map/ppermute | solution.py:107
